TPU v7x, 32 devices: a whole 2x2x4 slice. The times are simulated.
32 devices in a mesh: ctx: 8 (over y, x, core), dp: 4 (over z).
Axes of the slice: x: 2, y: 2, z: 4, core: 2. Of those that a mesh axis runs over, the one named last changes fastest.
Arguments:
- hidden_in: bfloat16 [4, 2048, 2048], P('dp', 'ctx'), may hold values from -6 to 6
- queries: bfloat16 [4, 2048, 2048], P('dp', 'ctx'), may hold values from -1000 to 1000
- norm_gain: bfloat16 [2048], replicated, may hold values from 0.099609375 to 1.8984375
- weight_store: bfloat16 [4, 2048, 512], P('dp', 'ctx'), may hold values from -0.125 to 0.125
- owners: int32 [2], replicated, may hold values from 0 to 3, as said below
- doc_lengths: int32 [4, 4], P('dp'), may hold values from 1 to 1024, 2048 in all within a row
Outputs:
- attended: bfloat16 [4, 2048, 2048], P('dp', 'ctx')
Inputs may be any that keep to these rules, and one draw needn't show every extreme that they name: `owners`: two different data ranks, one of them the last rank 4 - 1; the first owns the key projection, the second the value projection.
All inputs are finite; a program needn't handle non-finite values.
Results may differ from a plain program's by a relative error of at most 0.012.
Values may be sent and summed in bfloat16 or wider, within the bound.
No kernel may reach another device: no remote copies, remote signals or barrier semaphores. Data moves between devices by JAX's collectives and lax.ppermute only.
A program may use at most 64 MiB of HBM per device.

v0:
```python
import jax
import jax.numpy as jnp
from jax import lax
from jax.sharding import PartitionSpec as P

HS = 128
REACH = 4


def from_root(block, axis, owner):
    block = jnp.where(lax.axis_index(axis) == owner, block, jnp.zeros_like(block))
    return lax.psum(block, axis)


def from_behind(x, axis, by):
    size = lax.axis_size(axis)
    pairs = [(i, i + by) for i in range(size) if 0 <= i + by < size]
    return lax.ppermute(x, axis, pairs)


def find_starts(lengths, positions):
    ends = jnp.cumsum(lengths)
    starts = ends - lengths
    below = starts[None, :] <= positions[:, None]
    return jnp.max(jnp.where(below, starts[None, :], 0), axis=1)


def copy_owner(slot_rows, owner):
    return from_root(slot_rows, "dp", owner)


def local(hidden_in, queries, norm_gain, weight_store, owners, doc_lengths):
    tok_rows = hidden_in.shape[1]
    key_width = weight_store.shape[2]
    kv_heads = key_width // HS
    group = queries.shape[2] // key_width
    width_all = (REACH + 1) * tok_rows
    ctx_index = lax.axis_index("ctx")
    xf = hidden_in[0].astype(jnp.float32)
    scaled = (
        xf
        * lax.rsqrt(jnp.mean(xf * xf, axis=-1, keepdims=True) + 1e-05)
        * norm_gain.astype(jnp.float32)
    ).astype(jnp.bfloat16)
    own_slot = weight_store[0]
    key_part = copy_owner(own_slot, owners[0])
    value_part = copy_owner(own_slot, owners[1])
    key_sum = jnp.dot(
        scaled,
        lax.all_gather(key_part, "ctx", axis=0, tiled=True),
        preferred_element_type=jnp.float32,
    )
    value_sum = jnp.dot(
        scaled,
        lax.all_gather(value_part, "ctx", axis=0, tiled=True),
        preferred_element_type=jnp.float32,
    )
    kv_own = jnp.stack([key_sum.astype(jnp.bfloat16), value_sum.astype(jnp.bfloat16)])
    earlier = [from_behind(kv_own, "ctx", back) for back in range(REACH, 0, -1)]
    window = jnp.concatenate(earlier + [kv_own], axis=1)
    q_pos = ctx_index * tok_rows + jnp.arange(tok_rows, dtype=jnp.int32)
    k_pos = (ctx_index - REACH) * tok_rows + jnp.arange(width_all, dtype=jnp.int32)
    q_start = find_starts(doc_lengths[0], q_pos)
    allowed = (k_pos[None, :] >= q_start[:, None]) & (k_pos[None, :] <= q_pos[:, None])
    q_heads = jnp.transpose(queries[0].reshape(tok_rows, kv_heads, group, HS), (1, 2, 0, 3))
    k_heads = jnp.transpose(window[0].reshape(width_all, kv_heads, HS), (1, 0, 2))
    v_heads = jnp.transpose(window[1].reshape(width_all, kv_heads, HS), (1, 0, 2))
    inverse_root = 1.0 / jnp.sqrt(jnp.float32(HS))

    def one_head(args):
        q_one, k_one, v_one = args
        rows = q_one.reshape(group * tok_rows, HS)
        score = jnp.dot(rows, k_one.T, preferred_element_type=jnp.float32)
        score = score.reshape(group, tok_rows, width_all) * inverse_root
        score = jnp.where(allowed[None], score, jnp.float32(-1e30))
        top = jnp.max(score, axis=-1, keepdims=True)
        weight = jnp.exp(score - top)
        total = jnp.sum(weight, axis=-1)
        weight_b = weight.astype(jnp.bfloat16).reshape(group * tok_rows, width_all)
        summed = jnp.dot(weight_b, v_one, preferred_element_type=jnp.float32)
        summed = summed.reshape(group, tok_rows, HS)
        return (summed / total[..., None]).astype(jnp.bfloat16)

    outputs = lax.map(one_head, (q_heads, k_heads, v_heads))
    attended = jnp.transpose(outputs, (2, 0, 1, 3)).reshape(1, tok_rows, kv_heads * group * HS)
    return attended


def solution(mesh):
    return jax.shard_map(
        local,
        mesh=mesh,
        in_specs=(
            P("dp", "ctx", None),
            P("dp", "ctx", None),
            P(),
            P("dp", "ctx", None),
            P(),
            P("dp", None),
        ),
        out_specs=P("dp", "ctx", None),
        check_vma=False,
    )
```

profile of v0, /device:TPU:1, one launch (start us, length us, event | category | flops | bytes accessed | tf_op | source)
XLA Modules:
  0.0 198.7 jit_solution(8778680894563662250)
XLA Ops:
  6.5 1.4 fusion.36
  9.3 1.8 select_bitcast_fusion.1
  11.1 39.7 %all-reduce.3.cloned.1.call-done = (bf16[256,512]{1,0:T(8,128)(2,1)}, bf16[256,512]{1,0:T(8,128)(2,1)}) async-done(((bf16[256,512]{1,0:T(8,128)(2,1)}, bf16[256,512]{1,0:T(8,128)(2,1)}), (bf16[256,512]{1,0:T(8,128)(2,1)}, bf16[256,512]{1,0:T(8,128)(2,1)})) %all-reduce.3.cloned.1.call-update) | async-done | bytes 524304 | tf_op jit(solution)/shard_map/psum | solution.py:12
  53.4 28.6 %all-gather.3.cloned.1.call-done = bf16[2048,512]{1,0:T(8,128)(2,1)} async-done(((bf16[256,512]{1,0:T(8,128)(2,1)}), bf16[2048,512]{1,0:T(8,128)(2,1)}) %all-gather.3.cloned.1.call-update) | async-done | bytes 2097168 | tf_op jit(solution)/shard_map/all_gather | solution.py:50
  82.0 2.3 %fusion.30 = bf16[1,256,512]{2,1,0:T(8,128)(2,1)S(1)} fusion(bf16[2048,512]{1,0:T(8,128)(2,1)} %all-gather.3.cloned.1.call-done, bf16[1,256,2048]{2,1,0:T(8,128)(2,1)S(1)} %copy-done, f32[2048]{0:T(1024)S(1)} %convert_element_type.26, f32[256]{0:T(256)S(1)} %add_rsqrt_fusion), kind=kOutput, calls=%fused_computation.29 | convolution fusion | flops 539099136 | bytes 3417088 | tf_op jit(solution)/shard_map/dot_general | solution.py:48
  84.4 27.5 %all-gather.5.cloned.1.call-done = bf16[2048,512]{1,0:T(8,128)(2,1)} async-done(((bf16[256,512]{1,0:T(8,128)(2,1)}), bf16[2048,512]{1,0:T(8,128)(2,1)}) %all-gather.5.cloned.1.call-update) | async-done | bytes 2097168 | tf_op jit(solution)/shard_map/all_gather | solution.py:55
  111.8 2.3 %fusion.31 = bf16[1,256,512]{2,1,0:T(8,128)(2,1)S(1)} fusion(bf16[2048,512]{1,0:T(8,128)(2,1)} %all-gather.5.cloned.1.call-done, bf16[1,256,2048]{2,1,0:T(8,128)(2,1)S(1)} %copy-done, f32[2048]{0:T(1024)S(1)} %convert_element_type.26, f32[256]{0:T(256)S(1)} %add_rsqrt_fusion), kind=kOutput, calls=%fused_computation.30 | convolution fusion | flops 539099136 | bytes 3417088 | tf_op jit(solution)/shard_map/dot_general | solution.py:53
  115.7 3.8 %collective-permute-start = (bf16[2,256,512]{2,1,0:T(8,128)(2,1)}, bf16[2,256,512]{2,1,0:T(8,128)(2,1)}, u32[]{:S(2)}, u32[]{:S(2)}) collective-permute-start(bf16[2,256,512]{2,1,0:T(8,128)(2,1)} %pad_maximum_fusion), channel_id=1, source_target_pairs={{0,16},{4,20},{8,24},{12,28},{1,17},{5,21},{9,25},{13,29},{2,18},{... | collective-permute-start | bytes 1572872 | tf_op jit(solution)/shard_map/ppermute | solution.py:18
  119.5 2.1 %collective-permute-start.1 = (bf16[2,256,512]{2,1,0:T(8,128)(2,1)}, bf16[2,256,512]{2,1,0:T(8,128)(2,1)}, u32[]{:S(2)}, u32[]{:S(2)}) collective-permute-start(bf16[2,256,512]{2,1,0:T(8,128)(2,1)} %pad_maximum_fusion), channel_id=1, source_target_pairs={{0,12},{4,16},{8,20},{12,24},{16,28},{1,13},{5,17},{9,21},{13,25},... | collective-permute-start | bytes 1572872 | tf_op jit(solution)/shard_map/ppermute | solution.py:18
  121.6 2.9 %collective-permute-start.2 = (bf16[2,256,512]{2,1,0:T(8,128)(2,1)}, bf16[2,256,512]{2,1,0:T(8,128)(2,1)}, u32[]{:S(2)}, u32[]{:S(2)}) collective-permute-start(bf16[2,256,512]{2,1,0:T(8,128)(2,1)} %pad_maximum_fusion), channel_id=1, source_target_pairs={{0,8},{4,12},{8,16},{12,20},{16,24},{20,28},{1,9},{5,13},{9,17},{1... | collective-permute-start | bytes 1572872 | tf_op jit(solution)/shard_map/ppermute | solution.py:18
  124.5 1.9 collective-permute-start.3
  127.1 25.4 %collective-permute-done = bf16[2,256,512]{2,1,0:T(8,128)(2,1)} collective-permute-done((bf16[2,256,512]{2,1,0:T(8,128)(2,1)}, bf16[2,256,512]{2,1,0:T(8,128)(2,1)}, u32[]{:S(2)}, u32[]{:S(2)}) %collective-permute-start) | collective-permute-done | bytes 524320 | tf_op jit(solution)/shard_map/ppermute | solution.py:18
  153.6 5.2 %collective-permute-done.1 = bf16[2,256,512]{2,1,0:T(8,128)(2,1)} collective-permute-done((bf16[2,256,512]{2,1,0:T(8,128)(2,1)}, bf16[2,256,512]{2,1,0:T(8,128)(2,1)}, u32[]{:S(2)}, u32[]{:S(2)}) %collective-permute-start.1) | collective-permute-done | bytes 524320 | tf_op jit(solution)/shard_map/ppermute | solution.py:18
  163.4 3.6 %reshape_squeeze.10 = bf16[1280,4,128]{2,1,0:T(4,128)(2,1)} reshape(bf16[1,1280,512]{2,1,0:T(8,128)(2,1)} %get-tuple-element.96) | data formatting | bytes 2621440 | tf_op jit(solution)/shard_map/reshape;squeeze | solution.py:66
  168.2 3.1 %copy_bitcast_fusion = (bf16[4,1280,128]{2,1,0:T(8,128)(2,1)}, bf16[4,1280,128]{2,1,0:T(8,128)(2,1)S(1)}) fusion(bf16[1280,4,128]{2,1,0:T(4,128)(2,1)} %reshape_squeeze.11, bf16[1280,4,128]{2,1,0:T(4,128)(2,1)} %reshape_squeeze.10), kind=kLoop, calls=%fused_computation.25 | loop fusion | bytes 5242880 | tf_op jit(solution)/shard_map/transpose | solution.py:67
  171.3 18.5 %while.11 = (s32[]{:T(128)}, bf16[4,4,256,128]{3,2,1,0:T(8,128)(2,1)S(1)}, bf16[4,4,256,128]{2,3,1,0:T(8,128)(2,1)S(1)}, bf16[4,1280,128]{2,1,0:T(8,128)(2,1)S(1...) while((s32[]{:T(128)}, ...), condition=%wide.region_8.9_spmd.clone, body=%wide.region_5.8_spmd.clone.sunk | while | flops 681506816 | bytes 17593436 | solution.py:84
  173.9 2.0 %fusion.48 = bf16[4,4,256,128]{3,2,1,0:T(8,128)(2,1)S(1)} fusion(bf16[4,4,256,128]{3,2,1,0:T(8,128)(2,1)S(1)} %get-tuple-element.166, s32[]{:T(128)} %get-tuple-element.165, f32[4,256,1280]{2,1,0:T(8,128)S(1)} %get-tuple-element.154, f32[4,256]{1,0:T(4,128)S(1)} %get-tuple-element.155, bf16[4,1280,128]{2,1,0:T(8,128)(2,1)} %get-tuple-element.178, ...), kind=kOutput, calls=%fused_computation.11.clone.1 | convolution fusion | flops 338427904 | bytes 5841920 | tf_op jit(solution)/shard_map/while/body/eval_jaxpr/dot_general | solution.py:80
  176.2 1.3 fusion.46
  178.5 2.0 %fusion.48 = bf16[4,4,256,128]{3,2,1,0:T(8,128)(2,1)S(1)} fusion(bf16[4,4,256,128]{3,2,1,0:T(8,128)(2,1)S(1)} %get-tuple-element.166, s32[]{:T(128)} %get-tuple-element.165, f32[4,256,1280]{2,1,0:T(8,128)S(1)} %get-tuple-element.154, f32[4,256]{1,0:T(4,128)S(1)} %get-tuple-element.155, bf16[4,1280,128]{2,1,0:T(8,128)(2,1)} %get-tuple-element.178, ...), kind=kOutput, calls=%fused_computation.11.clone.1 | convolution fusion | flops 338427904 | bytes 5841920 | tf_op jit(solution)/shard_map/while/body/eval_jaxpr/dot_general | solution.py:80
  180.8 1.3 fusion.46
  183.1 2.0 %fusion.48 = bf16[4,4,256,128]{3,2,1,0:T(8,128)(2,1)S(1)} fusion(bf16[4,4,256,128]{3,2,1,0:T(8,128)(2,1)S(1)} %get-tuple-element.166, s32[]{:T(128)} %get-tuple-element.165, f32[4,256,1280]{2,1,0:T(8,128)S(1)} %get-tuple-element.154, f32[4,256]{1,0:T(4,128)S(1)} %get-tuple-element.155, bf16[4,1280,128]{2,1,0:T(8,128)(2,1)} %get-tuple-element.178, ...), kind=kOutput, calls=%fused_computation.11.clone.1 | convolution fusion | flops 338427904 | bytes 5841920 | tf_op jit(solution)/shard_map/while/body/eval_jaxpr/dot_general | solution.py:80
  185.5 1.3 fusion.46
  187.7 2.0 %fusion.48 = bf16[4,4,256,128]{3,2,1,0:T(8,128)(2,1)S(1)} fusion(bf16[4,4,256,128]{3,2,1,0:T(8,128)(2,1)S(1)} %get-tuple-element.166, s32[]{:T(128)} %get-tuple-element.165, f32[4,256,1280]{2,1,0:T(8,128)S(1)} %get-tuple-element.154, f32[4,256]{1,0:T(4,128)S(1)} %get-tuple-element.155, bf16[4,1280,128]{2,1,0:T(8,128)(2,1)} %get-tuple-element.178, ...), kind=kOutput, calls=%fused_computation.11.clone.1 | convolution fusion | flops 338427904 | bytes 5841920 | tf_op jit(solution)/shard_map/while/body/eval_jaxpr/dot_general | solution.py:80
  190.6 1.6 reshape.47
  (46 shorter events, 18.9 us)
Async XLA Ops:
  6.5 46.5 %copy-start = (bf16[1,256,2048]{2,1,0:T(8,128)(2,1)S(1)}, bf16[1,256,2048]{2,1,0:T(8,128)(2,1)}, u32[]{:S(2)}) copy-start(bf16[1,256,2048]{2,1,0:T(8,128)(2,1)} %param.8) | copy-start | bytes 3145732
  6.5 44.3 %all-reduce.3.cloned.1.call-start = ((), (), s32[]{:S(2)}) async-start(), calls=%async_computation.2 | async-start | bytes 1048576 | tf_op jit(solution)/shard_map/psum | solution.py:12
  11.1 70.9 %all-gather.3.cloned.1.call-start = ((), (), s32[]{:S(2)}) async-start(), calls=%async_computation | async-start | bytes 2359296 | tf_op jit(solution)/shard_map/all_gather | solution.py:50
  50.8 61.0 %all-gather.5.cloned.1.call-start = ((), (), s32[]{:S(2)}) async-start(), calls=%async_computation.1 | async-start | bytes 2359296 | tf_op jit(solution)/shard_map/all_gather | solution.py:55
  84.3 37.3 %copy-start.4 = (s32[1,4]{1,0:T(1,128)S(1)}, s32[1,4]{1,0:T(1,128)}, u32[]{:S(2)}) copy-start(s32[1,4]{1,0:T(1,128)} %param.13) | copy-start | bytes 52
  84.3 42.1 %copy-start.1 = (bf16[1,256,2048]{2,1,0:T(8,128)(2,1)S(1)}, bf16[1,256,2048]{2,1,0:T(8,128)(2,1)}, u32[]{:S(2)}) copy-start(bf16[1,256,2048]{2,1,0:T(8,128)(2,1)} %param.9) | copy-start | bytes 3145732
  114.2 0.7 copy-start.2
  115.7 36.8 %collective-permute-start = (bf16[2,256,512]{2,1,0:T(8,128)(2,1)}, bf16[2,256,512]{2,1,0:T(8,128)(2,1)}, u32[]{:S(2)}, u32[]{:S(2)}) collective-permute-start(bf16[2,256,512]{2,1,0:T(8,128)(2,1)} %pad_maximum_fusion), channel_id=1, source_target_pairs={{0,16},{4,20},{8,24},{12,28},{1,17},{5,21},{9,25},{13,29},{2,18},{... | collective-permute-start | bytes 1572872 | tf_op jit(solution)/shard_map/ppermute | solution.py:18
  119.5 39.3 %collective-permute-start.1 = (bf16[2,256,512]{2,1,0:T(8,128)(2,1)}, bf16[2,256,512]{2,1,0:T(8,128)(2,1)}, u32[]{:S(2)}, u32[]{:S(2)}) collective-permute-start(bf16[2,256,512]{2,1,0:T(8,128)(2,1)} %pad_maximum_fusion), channel_id=1, source_target_pairs={{0,12},{4,16},{8,20},{12,24},{16,28},{1,13},{5,17},{9,21},{13,25},... | collective-permute-start | bytes 1572872 | tf_op jit(solution)/shard_map/ppermute | solution.py:18
  121.6 38.3 %collective-permute-start.2 = (bf16[2,256,512]{2,1,0:T(8,128)(2,1)}, bf16[2,256,512]{2,1,0:T(8,128)(2,1)}, u32[]{:S(2)}, u32[]{:S(2)}) collective-permute-start(bf16[2,256,512]{2,1,0:T(8,128)(2,1)} %pad_maximum_fusion), channel_id=1, source_target_pairs={{0,8},{4,12},{8,16},{12,20},{16,24},{20,28},{1,9},{5,13},{9,17},{1... | collective-permute-start | bytes 1572872 | tf_op jit(solution)/shard_map/ppermute | solution.py:18
  124.5 36.5 %collective-permute-start.3 = (bf16[2,256,512]{2,1,0:T(8,128)(2,1)}, bf16[2,256,512]{2,1,0:T(8,128)(2,1)}, u32[]{:S(2)}, u32[]{:S(2)}) collective-permute-start(bf16[2,256,512]{2,1,0:T(8,128)(2,1)} %pad_maximum_fusion), channel_id=1, source_target_pairs={{0,4},{4,8},{8,12},{12,16},{16,20},{20,24},{24,28},{1,5},{5,9},{9,... | collective-permute-start | bytes 1572872 | tf_op jit(solution)/shard_map/ppermute | solution.py:18
  127.1 35.0 %copy-start.3 = (bf16[1,256,512]{2,1,0:T(8,128)(2,1)S(1)}, bf16[1,256,512]{2,1,0:T(8,128)(2,1)}, u32[]{:S(2)}) copy-start(bf16[1,256,512]{2,1,0:T(8,128)(2,1)} %copy-done.2) | copy-start | bytes 786436
Sparse Core Ops, SparseCore 0:
  11.2 39.5 all-reduce.2
  52.7 29.2 all-gather.2
  83.9 27.8 all-gather.4
where the time goes:
time: 199 us
  waiting for transfers between devices  127 us (64%)
  local copies, waits for them, and re-layouts  18.5 us (9%)
  matrix products  17.9 us (9%)
  between operations  14.6 us (7%)
  starting transfers between devices  10.8 us (5%)
  other arithmetic  9.72 us (5%)
    psum x1, waiting for transfers between devices, from_root(): return lax.psum(block, axis)  39.7 us
    ppermute x4, waiting for transfers between devices, from_behind(): return lax.ppermute(x, axis, pairs)  30.6 us
    all_gather x1, waiting for transfers between devices, local(): lax.all_gather(key_part, 'ctx', axis=0, tiled=True)  28.6 us
    all_gather x1, waiting for transfers between devices, local(): lax.all_gather(value_part, 'ctx', axis=0, tiled=True)  27.5 us
    ppermute x4, starting transfers between devices, from_behind(): return lax.ppermute(x, axis, pairs)  10.7 us
    dot_general x4, matrix products, one_head(): summed = jnp.dot(weight_b, v_one, preferred_element_type=jnp.float32)  8.07 us
    unnamed x15, local copies, waits for them, and re-layouts  5.55 us
    dot_general x4, matrix products, one_head(): score = jnp.dot(rows, k_one.T, preferred_element_type=jnp.float32)  5.14 us
  transfers between devices with their start and end apart: 7, of which 5 were waited for; matrix products, arithmetic and copies ran while one was open for 4% of the time, Pallas kernels for 0%

commit v1 on v0

--- a/solution.py
+++ b/solution.py
@@ -5,6 +5,28 @@
 
 HS = 128
 REACH = 4
+
+
+def in_order(blocks, dim):
+    blocks = jnp.moveaxis(blocks, 0, dim)
+    shape = blocks.shape
+    return blocks.reshape(*shape[:dim], shape[dim] * shape[dim + 1], *shape[dim + 2 :])
+
+
+def ring_gather(array, axis, dim):
+    size = lax.axis_size(axis)
+    pairs = [(i, (i + 1) % size) for i in range(size)]
+    back = [(b, a) for a, b in pairs]
+    lower, upper = ([], [])
+    for step in range(size - 1):
+        if step % 2 == 0:
+            lower.append(lax.ppermute(lower[-1] if lower else array, axis, pairs))
+        else:
+            upper.append(lax.ppermute(upper[-1] if upper else array, axis, back))
+    blocks = jnp.stack([*lower[::-1], array, *upper])
+    shift = lax.axis_index(axis) - len(lower)
+    blocks = blocks[(jnp.arange(size) - shift) % size]
+    return in_order(blocks, dim)
 
 
 def from_root(block, axis, owner):
@@ -51,9 +73,7 @@
         preferred_element_type=jnp.float32,
     )
     value_sum = jnp.dot(
-        scaled,
-        lax.all_gather(value_part, "ctx", axis=0, tiled=True),
-        preferred_element_type=jnp.float32,
+        scaled, ring_gather(value_part, "ctx", 0), preferred_element_type=jnp.float32
     )
     kv_own = jnp.stack([key_sum.astype(jnp.bfloat16), value_sum.astype(jnp.bfloat16)])
     earlier = [from_behind(kv_own, "ctx", back) for back in range(REACH, 0, -1)]

time: 199 us -> 183 us (0.920)
  waiting for transfers between devices: 127 us -> 87 us
  starting transfers between devices: 10.8 us -> 28.9 us
  local copies, waits for them, and re-layouts: 18.5 us -> 24.7 us
    all_gather x1, waiting for transfers between devices: 28.6 us -> 0.02 us  [local(): lax.all_gather(key_part, 'ctx', axis=0, tiled=True)]
    all_gather x1 -> x0, waiting for transfers between devices: 27.5 us -> none  [local(): lax.all_gather(value_part, 'ctx', axis=0, tiled=True)]
    ppermute x0 -> x7, waiting for transfers between devices: none -> 21.1 us  [the longest x4 11.2 us: ring_gather(): lower.append(lax.ppermute(lower[-1] if lower else array, axis, pairs))]
    ppermute x0 -> x7, starting transfers between devices: none -> 12.9 us  [the longest x4 10.2 us: ring_gather(): lower.append(lax.ppermute(lower[-1] if lower else array, axis, pairs))]
    ppermute x4, starting transfers between devices: 10.7 us -> 16 us  [from_behind(): return lax.ppermute(x, axis, pairs)]
    ppermute x4, waiting for transfers between devices: 30.6 us -> 26.2 us  [from_behind(): return lax.ppermute(x, axis, pairs)]
    unnamed x15 -> x40, local copies, waits for them, and re-layouts: 5.55 us -> 9.81 us
  transfers between devices with their start and end apart: 7 -> 13, of which waited for: 5 -> 9; matrix products, arithmetic and copies ran while one was open for 4% -> 7% of each run, Pallas kernels for 0% -> 0%
where the time goes in v1:
time: 183 us; the launch traced here: 182 us
  waiting for transfers between devices  87 us (48%)
  starting transfers between devices  28.9 us (16%)
  local copies, waits for them, and re-layouts  24.7 us (13%)
  matrix products  18 us (10%)
  between operations  15 us (8%)
  other arithmetic  8.44 us (5%)
    psum x1, waiting for transfers between devices, from_root(): return lax.psum(block, axis)  39.7 us
    ppermute x4, waiting for transfers between devices, from_behind(): return lax.ppermute(x, axis, pairs)  26.2 us
    ppermute x4, starting transfers between devices, from_behind(): return lax.ppermute(x, axis, pairs)  16 us
    ppermute x4, waiting for transfers between devices, ring_gather(): lower.append(lax.ppermute(lower[-1] if lower else array, axis, pairs))  11.2 us
    ppermute x4, starting transfers between devices, ring_gather(): lower.append(lax.ppermute(lower[-1] if lower else array, axis, pairs))  10.2 us
    ppermute x3, waiting for transfers between devices, ring_gather(): upper.append(lax.ppermute(upper[-1] if upper else array, axis, back))  9.88 us
    unnamed x40, local copies, waits for them, and re-layouts  9.81 us
    dot_general x4, matrix products, one_head(): summed = jnp.dot(weight_b, v_one, preferred_element_type=jnp.float32)  8.07 us
  transfers between devices with their start and end apart: 13, of which 9 were waited for; matrix products, arithmetic and copies ran while one was open for 7% of the time, Pallas kernels for 0%

profile of v1, /device:TPU:1, one launch (start us, length us, event | category | flops | bytes accessed | tf_op | source)
XLA Modules:
  0.0 182.2 jit_solution(14895654219731491559)
XLA Ops:
  11.0 39.7 %all-reduce.3.cloned.1.call-done = (bf16[256,512]{1,0:T(8,128)(2,1)}, bf16[256,512]{1,0:T(8,128)(2,1)}) async-done(((bf16[256,512]{1,0:T(8,128)(2,1)}, bf16[256,512]{1,0:T(8,128)(2,1)}), (bf16[256,512]{1,0:T(8,128)(2,1)}, bf16[256,512]{1,0:T(8,128)(2,1)})) %all-reduce.3.cloned.1.call-update) | async-done | bytes 524304 | tf_op jit(solution)/shard_map/psum | solution.py:34
  50.7 2.8 %collective-permute-start = (bf16[256,512]{1,0:T(8,128)(2,1)}, bf16[256,512]{1,0:T(8,128)(2,1)S(1)}, u32[]{:S(2)}, u32[]{:S(2)}) collective-permute-start(bf16[256,512]{1,0:T(8,128)(2,1)} %get-tuple-element.91), channel_id=1, source_target_pairs={{0,4},{4,8},{8,12},{12,16},{16,20},{20,24},{24,28},{28,0},{1,5},{5... | collective-permute-start | bytes 786440 | tf_op jit(solution)/shard_map/ppermute | solution.py:23
  53.6 3.6 %collective-permute-done = bf16[256,512]{1,0:T(8,128)(2,1)S(1)} collective-permute-done((bf16[256,512]{1,0:T(8,128)(2,1)}, bf16[256,512]{1,0:T(8,128)(2,1)S(1)}, u32[]{:S(2)}, u32[]{:S(2)}) %collective-permute-start) | collective-permute-done | bytes 262176 | tf_op jit(solution)/shard_map/ppermute | solution.py:23
  57.2 2.4 %collective-permute-start.1 = (bf16[256,512]{1,0:T(8,128)(2,1)S(1)}, bf16[256,512]{1,0:T(8,128)(2,1)S(1)}, u32[]{:S(2)}, u32[]{:S(2)}) collective-permute-start(bf16[256,512]{1,0:T(8,128)(2,1)S(1)} %collective-permute-done), channel_id=1, source_target_pairs={{0,4},{4,8},{8,12},{12,16},{16,20},{20,24},{24,28},{28,0},{1,5},{5... | collective-permute-start | bytes 786440 | tf_op jit(solution)/shard_map/ppermute | solution.py:23
  59.6 6.3 %collective-permute-done.1 = bf16[256,512]{1,0:T(8,128)(2,1)S(1)} collective-permute-done((bf16[256,512]{1,0:T(8,128)(2,1)S(1)}, bf16[256,512]{1,0:T(8,128)(2,1)S(1)}, u32[]{:S(2)}, u32[]{:S(2)}) %collective-permute-start.1) | collective-permute-done | bytes 262176 | tf_op jit(solution)/shard_map/ppermute | solution.py:23
  65.8 2.5 %collective-permute-start.2 = (bf16[256,512]{1,0:T(8,128)(2,1)S(1)}, bf16[256,512]{1,0:T(8,128)(2,1)S(1)}, u32[]{:S(2)}, u32[]{:S(2)}) collective-permute-start(bf16[256,512]{1,0:T(8,128)(2,1)S(1)} %collective-permute-done.1), channel_id=1, source_target_pairs={{0,4},{4,8},{8,12},{12,16},{16,20},{20,24},{24,28},{28,0},{1,5},{5... | collective-permute-start | bytes 786440 | tf_op jit(solution)/shard_map/ppermute | solution.py:23
  68.6 2.4 %collective-permute-done.4 = bf16[256,512]{1,0:T(8,128)(2,1)S(1)} collective-permute-done((bf16[256,512]{1,0:T(8,128)(2,1)}, bf16[256,512]{1,0:T(8,128)(2,1)S(1)}, u32[]{:S(2)}, u32[]{:S(2)}) %collective-permute-start.4) | collective-permute-done | bytes 262176 | tf_op jit(solution)/shard_map/ppermute | solution.py:25
  71.6 2.5 %collective-permute-start.3 = (bf16[256,512]{1,0:T(8,128)(2,1)S(1)}, bf16[256,512]{1,0:T(8,128)(2,1)}, u32[]{:S(2)}, u32[]{:S(2)}) collective-permute-start(bf16[256,512]{1,0:T(8,128)(2,1)S(1)} %collective-permute-done.2), channel_id=1, source_target_pairs={{0,4},{4,8},{8,12},{12,16},{16,20},{20,24},{24,28},{28,0},{1,5},{5... | collective-permute-start | bytes 786440 | tf_op jit(solution)/shard_map/ppermute | solution.py:23
  74.3 7.5 %collective-permute-done.5 = bf16[256,512]{1,0:T(8,128)(2,1)} collective-permute-done((bf16[256,512]{1,0:T(8,128)(2,1)S(1)}, bf16[256,512]{1,0:T(8,128)(2,1)}, u32[]{:S(2)}, u32[]{:S(2)}) %collective-permute-start.5) | collective-permute-done | bytes 262176 | tf_op jit(solution)/shard_map/ppermute | solution.py:25
  81.8 2.7 %collective-permute-start.6 = (bf16[256,512]{1,0:T(8,128)(2,1)}, bf16[256,512]{1,0:T(8,128)(2,1)S(1)}, u32[]{:S(2)}, u32[]{:S(2)}) collective-permute-start(bf16[256,512]{1,0:T(8,128)(2,1)} %collective-permute-done.5), channel_id=1, source_target_pairs={{4,0},{8,4},{12,8},{16,12},{20,16},{24,20},{28,24},{0,28},{5,1},{9... | collective-permute-start | bytes 786440 | tf_op jit(solution)/shard_map/ppermute | solution.py:25
  92.3 2.3 %fusion.35 = bf16[1,256,512]{2,1,0:T(8,128)(2,1)S(1)} fusion(bf16[2048,512]{1,0:T(8,128)(2,1)} %bitcast.86, bf16[1,256,2048]{2,1,0:T(8,128)(2,1)S(1)} %copy-done, f32[2048]{0:T(1024)S(1)} %convert_element_type.34, f32[256]{0:T(256)S(1)} %add_rsqrt_fusion), kind=kOutput, calls=%fused_computation.35 | convolution fusion | flops 539099136 | bytes 3417088 | tf_op jit(solution)/shard_map/dot_general | solution.py:75
  94.7 2.5 %fusion.34 = bf16[1,256,512]{2,1,0:T(8,128)(2,1)S(1)} fusion(bf16[2048,512]{1,0:T(8,128)(2,1)} %all-gather.2.cloned.1.call-done, bf16[1,256,2048]{2,1,0:T(8,128)(2,1)S(1)} %copy-done, f32[2048]{0:T(1024)S(1)} %convert_element_type.34, f32[256]{0:T(256)S(1)} %add_rsqrt_fusion), kind=kOutput, calls=%fused_computation.34 | convolution fusion | flops 539099136 | bytes 3417088 | tf_op jit(solution)/shard_map/dot_general | solution.py:70
  98.0 4.6 %collective-permute-start.7 = (bf16[2,256,512]{2,1,0:T(8,128)(2,1)}, bf16[2,256,512]{2,1,0:T(8,128)(2,1)}, u32[]{:S(2)}, u32[]{:S(2)}) collective-permute-start(bf16[2,256,512]{2,1,0:T(8,128)(2,1)} %pad_maximum_fusion), channel_id=1, source_target_pairs={{0,16},{4,20},{8,24},{12,28},{1,17},{5,21},{9,25},{13,29},{2,18},{... | collective-permute-start | bytes 1572872 | tf_op jit(solution)/shard_map/ppermute | solution.py:40
  102.6 6.8 %collective-permute-start.8 = (bf16[2,256,512]{2,1,0:T(8,128)(2,1)}, bf16[2,256,512]{2,1,0:T(8,128)(2,1)}, u32[]{:S(2)}, u32[]{:S(2)}) collective-permute-start(bf16[2,256,512]{2,1,0:T(8,128)(2,1)} %pad_maximum_fusion), channel_id=1, source_target_pairs={{0,12},{4,16},{8,20},{12,24},{16,28},{1,13},{5,17},{9,21},{13,25},... | collective-permute-start | bytes 1572872 | tf_op jit(solution)/shard_map/ppermute | solution.py:40
  109.5 2.1 %collective-permute-start.9 = (bf16[2,256,512]{2,1,0:T(8,128)(2,1)}, bf16[2,256,512]{2,1,0:T(8,128)(2,1)}, u32[]{:S(2)}, u32[]{:S(2)}) collective-permute-start(bf16[2,256,512]{2,1,0:T(8,128)(2,1)} %pad_maximum_fusion), channel_id=1, source_target_pairs={{0,8},{4,12},{8,16},{12,20},{16,24},{20,28},{1,9},{5,13},{9,17},{1... | collective-permute-start | bytes 1572872 | tf_op jit(solution)/shard_map/ppermute | solution.py:40
  111.6 2.5 %collective-permute-start.10 = (bf16[2,256,512]{2,1,0:T(8,128)(2,1)}, bf16[2,256,512]{2,1,0:T(8,128)(2,1)}, u32[]{:S(2)}, u32[]{:S(2)}) collective-permute-start(bf16[2,256,512]{2,1,0:T(8,128)(2,1)} %pad_maximum_fusion), channel_id=1, source_target_pairs={{0,4},{4,8},{8,12},{12,16},{16,20},{20,24},{24,28},{1,5},{5,9},{9,... | collective-permute-start | bytes 1572872 | tf_op jit(solution)/shard_map/ppermute | solution.py:40
  114.7 18.2 %collective-permute-done.7 = bf16[2,256,512]{2,1,0:T(8,128)(2,1)} collective-permute-done((bf16[2,256,512]{2,1,0:T(8,128)(2,1)}, bf16[2,256,512]{2,1,0:T(8,128)(2,1)}, u32[]{:S(2)}, u32[]{:S(2)}) %collective-permute-start.7) | collective-permute-done | bytes 524320 | tf_op jit(solution)/shard_map/ppermute | solution.py:40
  133.9 8.0 %collective-permute-done.8 = bf16[2,256,512]{2,1,0:T(8,128)(2,1)} collective-permute-done((bf16[2,256,512]{2,1,0:T(8,128)(2,1)}, bf16[2,256,512]{2,1,0:T(8,128)(2,1)}, u32[]{:S(2)}, u32[]{:S(2)}) %collective-permute-start.8) | collective-permute-done | bytes 524320 | tf_op jit(solution)/shard_map/ppermute | solution.py:40
  146.5 3.6 %reshape_squeeze.10 = bf16[1280,4,128]{2,1,0:T(4,128)(2,1)} reshape(bf16[1,1280,512]{2,1,0:T(8,128)(2,1)} %get-tuple-element.96) | data formatting | bytes 2621440 | tf_op jit(solution)/shard_map/reshape;squeeze | solution.py:86
  151.3 3.1 %copy_bitcast_fusion = (bf16[4,1280,128]{2,1,0:T(8,128)(2,1)}, bf16[4,1280,128]{2,1,0:T(8,128)(2,1)S(1)}) fusion(bf16[1280,4,128]{2,1,0:T(4,128)(2,1)} %reshape_squeeze.11, bf16[1280,4,128]{2,1,0:T(4,128)(2,1)} %reshape_squeeze.10), kind=kLoop, calls=%fused_computation.30 | loop fusion | bytes 5242880 | tf_op jit(solution)/shard_map/transpose | solution.py:87
  154.4 18.5 %while.11 = (s32[]{:T(128)}, bf16[4,4,256,128]{3,2,1,0:T(8,128)(2,1)S(1)}, bf16[4,4,256,128]{2,3,1,0:T(8,128)(2,1)S(1)}, bf16[4,1280,128]{2,1,0:T(8,128)(2,1)S(1...) while((s32[]{:T(128)}, ...), condition=%wide.region_8.9_spmd.clone, body=%wide.region_5.8_spmd.clone.sunk | while | flops 681506816 | bytes 17593436 | solution.py:104
  161.6 2.0 %fusion.59 = bf16[4,4,256,128]{3,2,1,0:T(8,128)(2,1)S(1)} fusion(bf16[4,4,256,128]{3,2,1,0:T(8,128)(2,1)S(1)} %get-tuple-element.166, s32[]{:T(128)} %get-tuple-element.165, f32[4,256,1280]{2,1,0:T(8,128)S(1)} %get-tuple-element.154, f32[4,256]{1,0:T(4,128)S(1)} %get-tuple-element.155, bf16[4,1280,128]{2,1,0:T(8,128)(2,1)} %get-tuple-element.178, ...), kind=kOutput, calls=%fused_computation.12.clone.1 | convolution fusion | flops 338427904 | bytes 5841920 | tf_op jit(solution)/shard_map/while/body/eval_jaxpr/dot_general | solution.py:100
  166.2 2.0 %fusion.59 = bf16[4,4,256,128]{3,2,1,0:T(8,128)(2,1)S(1)} fusion(bf16[4,4,256,128]{3,2,1,0:T(8,128)(2,1)S(1)} %get-tuple-element.166, s32[]{:T(128)} %get-tuple-element.165, f32[4,256,1280]{2,1,0:T(8,128)S(1)} %get-tuple-element.154, f32[4,256]{1,0:T(4,128)S(1)} %get-tuple-element.155, bf16[4,1280,128]{2,1,0:T(8,128)(2,1)} %get-tuple-element.178, ...), kind=kOutput, calls=%fused_computation.12.clone.1 | convolution fusion | flops 338427904 | bytes 5841920 | tf_op jit(solution)/shard_map/while/body/eval_jaxpr/dot_general | solution.py:100
  170.9 2.0 %fusion.59 = bf16[4,4,256,128]{3,2,1,0:T(8,128)(2,1)S(1)} fusion(bf16[4,4,256,128]{3,2,1,0:T(8,128)(2,1)S(1)} %get-tuple-element.166, s32[]{:T(128)} %get-tuple-element.165, f32[4,256,1280]{2,1,0:T(8,128)S(1)} %get-tuple-element.154, f32[4,256]{1,0:T(4,128)S(1)} %get-tuple-element.155, bf16[4,1280,128]{2,1,0:T(8,128)(2,1)} %get-tuple-element.178, ...), kind=kOutput, calls=%fused_computation.12.clone.1 | convolution fusion | flops 338427904 | bytes 5841920 | tf_op jit(solution)/shard_map/while/body/eval_jaxpr/dot_general | solution.py:100
  (86 shorter events, 35.1 us)
Async XLA Ops:
  6.5 61.8 %copy-start = (bf16[1,256,2048]{2,1,0:T(8,128)(2,1)S(1)}, bf16[1,256,2048]{2,1,0:T(8,128)(2,1)}, u32[]{:S(2)}) copy-start(bf16[1,256,2048]{2,1,0:T(8,128)(2,1)} %param.8) | copy-start | bytes 3145732
  6.5 67.6 %copy-start.12 = (bf16[2048]{0:T(1024)(128)(2,1)S(1)}, bf16[2048]{0:T(1024)(128)(2,1)}, u32[]{:S(2)}) copy-start(bf16[2048]{0:T(1024)(128)(2,1)} %param.10) | copy-start | bytes 12292
  6.5 67.6 %copy-start.13 = (s32[1,4]{1,0:T(1,128)S(1)}, s32[1,4]{1,0:T(1,128)}, u32[]{:S(2)}) copy-start(s32[1,4]{1,0:T(1,128)} %param.13) | copy-start | bytes 52
  6.5 44.2 %all-reduce.3.cloned.1.call-start = ((), (), s32[]{:S(2)}) async-start(), calls=%async_computation.1 | async-start | bytes 1048576 | tf_op jit(solution)/shard_map/psum | solution.py:34
  11.0 83.7 %all-gather.2.cloned.1.call-start = ((), (), s32[]{:S(2)}) async-start(), calls=%async_computation | async-start | bytes 2359296 | tf_op jit(solution)/shard_map/all_gather | solution.py:72
  50.7 38.5 %copy-start.6 = (bf16[256,512]{1,0:T(8,128)(2,1)S(1)}, bf16[256,512]{1,0:T(8,128)(2,1)}, u32[]{:S(2)}) copy-start(bf16[256,512]{1,0:T(8,128)(2,1)} %get-tuple-element.91) | copy-start | bytes 786436
  50.7 6.5 %collective-permute-start = (bf16[256,512]{1,0:T(8,128)(2,1)}, bf16[256,512]{1,0:T(8,128)(2,1)S(1)}, u32[]{:S(2)}, u32[]{:S(2)}) collective-permute-start(bf16[256,512]{1,0:T(8,128)(2,1)} %get-tuple-element.91), channel_id=1, source_target_pairs={{0,4},{4,8},{8,12},{12,16},{16,20},{20,24},{24,28},{28,0},{1,5},{5... | collective-permute-start | bytes 786440 | tf_op jit(solution)/shard_map/ppermute | solution.py:23
  57.2 27.3 %copy-start.7 = (bf16[256,512]{1,0:T(8,128)(2,1)}, bf16[256,512]{1,0:T(8,128)(2,1)S(1)}, u32[]{:S(2)}) copy-start(bf16[256,512]{1,0:T(8,128)(2,1)S(1)} %collective-permute-done) | copy-start | bytes 786436
  57.2 8.6 %collective-permute-start.1 = (bf16[256,512]{1,0:T(8,128)(2,1)S(1)}, bf16[256,512]{1,0:T(8,128)(2,1)S(1)}, u32[]{:S(2)}, u32[]{:S(2)}) collective-permute-start(bf16[256,512]{1,0:T(8,128)(2,1)S(1)} %collective-permute-done), channel_id=1, source_target_pairs={{0,4},{4,8},{8,12},{12,16},{16,20},{20,24},{24,28},{28,0},{1,5},{5... | collective-permute-start | bytes 786440 | tf_op jit(solution)/shard_map/ppermute | solution.py:23
  59.6 11.5 %collective-permute-start.4 = (bf16[256,512]{1,0:T(8,128)(2,1)}, bf16[256,512]{1,0:T(8,128)(2,1)S(1)}, u32[]{:S(2)}, u32[]{:S(2)}) collective-permute-start(bf16[256,512]{1,0:T(8,128)(2,1)} %get-tuple-element.91), channel_id=1, source_target_pairs={{4,0},{8,4},{12,8},{16,12},{20,16},{24,20},{28,24},{0,28},{5,1},{9... | collective-permute-start | bytes 786440 | tf_op jit(solution)/shard_map/ppermute | solution.py:25
  65.8 18.7 %copy-start.8 = (bf16[256,512]{1,0:T(8,128)(2,1)}, bf16[256,512]{1,0:T(8,128)(2,1)S(1)}, u32[]{:S(2)}) copy-start(bf16[256,512]{1,0:T(8,128)(2,1)S(1)} %collective-permute-done.1) | copy-start | bytes 786436
  65.8 5.8 %collective-permute-start.2 = (bf16[256,512]{1,0:T(8,128)(2,1)S(1)}, bf16[256,512]{1,0:T(8,128)(2,1)S(1)}, u32[]{:S(2)}, u32[]{:S(2)}) collective-permute-start(bf16[256,512]{1,0:T(8,128)(2,1)S(1)} %collective-permute-done.1), channel_id=1, source_target_pairs={{0,4},{4,8},{8,12},{12,16},{16,20},{20,24},{24,28},{28,0},{1,5},{5... | collective-permute-start | bytes 786440 | tf_op jit(solution)/shard_map/ppermute | solution.py:23
  71.0 13.5 %copy-start.9 = (bf16[256,512]{1,0:T(8,128)(2,1)}, bf16[256,512]{1,0:T(8,128)(2,1)S(1)}, u32[]{:S(2)}) copy-start(bf16[256,512]{1,0:T(8,128)(2,1)S(1)} %collective-permute-done.4) | copy-start | bytes 786436
  71.0 10.8 %collective-permute-start.5 = (bf16[256,512]{1,0:T(8,128)(2,1)S(1)}, bf16[256,512]{1,0:T(8,128)(2,1)}, u32[]{:S(2)}, u32[]{:S(2)}) collective-permute-start(bf16[256,512]{1,0:T(8,128)(2,1)S(1)} %collective-permute-done.4), channel_id=1, source_target_pairs={{4,0},{8,4},{12,8},{16,12},{20,16},{24,20},{28,24},{0,28},{5,1},{9... | collective-permute-start | bytes 786440 | tf_op jit(solution)/shard_map/ppermute | solution.py:25
  71.6 13.7 %collective-permute-start.3 = (bf16[256,512]{1,0:T(8,128)(2,1)S(1)}, bf16[256,512]{1,0:T(8,128)(2,1)}, u32[]{:S(2)}, u32[]{:S(2)}) collective-permute-start(bf16[256,512]{1,0:T(8,128)(2,1)S(1)} %collective-permute-done.2), channel_id=1, source_target_pairs={{0,4},{4,8},{8,12},{12,16},{16,20},{20,24},{24,28},{28,0},{1,5},{5... | collective-permute-start | bytes 786440 | tf_op jit(solution)/shard_map/ppermute | solution.py:23
  81.8 8.5 %collective-permute-start.6 = (bf16[256,512]{1,0:T(8,128)(2,1)}, bf16[256,512]{1,0:T(8,128)(2,1)S(1)}, u32[]{:S(2)}, u32[]{:S(2)}) collective-permute-start(bf16[256,512]{1,0:T(8,128)(2,1)} %collective-permute-done.5), channel_id=1, source_target_pairs={{4,0},{8,4},{12,8},{16,12},{20,16},{24,20},{28,24},{0,28},{5,1},{9... | collective-permute-start | bytes 786440 | tf_op jit(solution)/shard_map/ppermute | solution.py:25
  94.6 19.4 %copy-start.1 = (bf16[1,256,2048]{2,1,0:T(8,128)(2,1)S(1)}, bf16[1,256,2048]{2,1,0:T(8,128)(2,1)}, u32[]{:S(2)}) copy-start(bf16[1,256,2048]{2,1,0:T(8,128)(2,1)} %param.9) | copy-start | bytes 3145732
  97.2 16.9 %copy-start.4 = (bf16[1,256,512]{2,1,0:T(8,128)(2,1)}, bf16[1,256,512]{2,1,0:T(8,128)(2,1)S(1)}, u32[]{:S(2)}) copy-start(bf16[1,256,512]{2,1,0:T(8,128)(2,1)S(1)} %fusion.34) | copy-start | bytes 786436
  98.0 34.8 %collective-permute-start.7 = (bf16[2,256,512]{2,1,0:T(8,128)(2,1)}, bf16[2,256,512]{2,1,0:T(8,128)(2,1)}, u32[]{:S(2)}, u32[]{:S(2)}) collective-permute-start(bf16[2,256,512]{2,1,0:T(8,128)(2,1)} %pad_maximum_fusion), channel_id=1, source_target_pairs={{0,16},{4,20},{8,24},{12,28},{1,17},{5,21},{9,25},{13,29},{2,18},{... | collective-permute-start | bytes 1572872 | tf_op jit(solution)/shard_map/ppermute | solution.py:40
  102.6 39.3 %collective-permute-start.8 = (bf16[2,256,512]{2,1,0:T(8,128)(2,1)}, bf16[2,256,512]{2,1,0:T(8,128)(2,1)}, u32[]{:S(2)}, u32[]{:S(2)}) collective-permute-start(bf16[2,256,512]{2,1,0:T(8,128)(2,1)} %pad_maximum_fusion), channel_id=1, source_target_pairs={{0,12},{4,16},{8,20},{12,24},{16,28},{1,13},{5,17},{9,21},{13,25},... | collective-permute-start | bytes 1572872 | tf_op jit(solution)/shard_map/ppermute | solution.py:40
  109.5 33.6 %collective-permute-start.9 = (bf16[2,256,512]{2,1,0:T(8,128)(2,1)}, bf16[2,256,512]{2,1,0:T(8,128)(2,1)}, u32[]{:S(2)}, u32[]{:S(2)}) collective-permute-start(bf16[2,256,512]{2,1,0:T(8,128)(2,1)} %pad_maximum_fusion), channel_id=1, source_target_pairs={{0,8},{4,12},{8,16},{12,20},{16,24},{20,28},{1,9},{5,13},{9,17},{1... | collective-permute-start | bytes 1572872 | tf_op jit(solution)/shard_map/ppermute | solution.py:40
  111.6 32.6 %collective-permute-start.10 = (bf16[2,256,512]{2,1,0:T(8,128)(2,1)}, bf16[2,256,512]{2,1,0:T(8,128)(2,1)}, u32[]{:S(2)}, u32[]{:S(2)}) collective-permute-start(bf16[2,256,512]{2,1,0:T(8,128)(2,1)} %pad_maximum_fusion), channel_id=1, source_target_pairs={{0,4},{4,8},{8,12},{12,16},{16,20},{20,24},{24,28},{1,5},{5,9},{9,... | collective-permute-start | bytes 1572872 | tf_op jit(solution)/shard_map/ppermute | solution.py:40
  114.7 30.5 %copy-start.3 = (bf16[1,256,512]{2,1,0:T(8,128)(2,1)S(1)}, bf16[1,256,512]{2,1,0:T(8,128)(2,1)}, u32[]{:S(2)}) copy-start(bf16[1,256,512]{2,1,0:T(8,128)(2,1)} %copy-done.2) | copy-start | bytes 786436
  114.7 30.5 %copy-start.5 = (bf16[1,256,512]{2,1,0:T(8,128)(2,1)S(1)}, bf16[1,256,512]{2,1,0:T(8,128)(2,1)}, u32[]{:S(2)}) copy-start(bf16[1,256,512]{2,1,0:T(8,128)(2,1)} %copy-done.4) | copy-start | bytes 786436
  (3 other events, 19.4 us)
Sparse Core Ops, SparseCore 0:
  11.1 39.5 all-reduce.2
  52.6 34.6 all-gather.1
